TPU v7x, 32 devices: a whole 2x2x4 slice. The times are simulated.
32 devices in a mesh: gx: 8 (over y, x, core), gy: 4 (over z).
Axes of the slice: x: 2, y: 2, z: 4, core: 2. Of those that a mesh axis runs over, the one named last changes fastest.
Arguments:
- velocity: float32 [3, 256, 256, 256], P(None, 'gx', 'gy'), may hold values from -4 to 4
- fluid_noise: float32 [3, 256, 256, 256], P(None, 'gx', 'gy'), may hold values from -3 to 3
- cell: int32 [3, 4096], P(None, ('gx', 'gy')), may hold values from 0 to 255, as said below
- offset: float32 [3, 4096], P(None, ('gx', 'gy')), may hold values from 0 to 1
- colloid_velocity: float32 [3, 4096], P(None, ('gx', 'gy')), may hold values from -5 to 5
- particle_noise: float32 [3, 4096], P(None, ('gx', 'gy')), may hold values from -5 to 5
- counts: int32 [32], P(('gx', 'gy')), may hold values from 32 to 128, as said below
Outputs:
- new_velocity: float32 [3, 256, 256, 256], P(None, 'gx', 'gy')
- colloid_force: float32 [3, 4096], P(None, ('gx', 'gy'))
- colloid_drift: float32 [3, 4096], P(None, ('gx', 'gy'))
Inputs may be any that keep to these rules, and one draw needn't show every extreme that they name: `cell`: rows b * 128 to (b + 1) * 128 - 1 form block b. Their first coordinate lies from (b // 4) * 32 up to 32 more, their second from (b mod (4)) * 64 up to 64 more. `counts`: rows of a block at or beyond its count are padding. One block is full in every draw.
All inputs are finite; a program needn't handle non-finite values.
Results may differ from a plain program's by a relative error of at most 0.0003.
Values sent between devices are 32-bit elements; how exact they have to be, the bound alone decides.
No kernel may reach another device: no remote copies, remote signals or barrier semaphores. Data moves between devices by JAX's collectives and lax.ppermute only.
A program may use at most 192 MiB of HBM per device.

v0:
```python
import math
import jax
import jax.numpy as jnp
from jax import lax
from jax.sharding import PartitionSpec as P

drag_rate = 1.0
time_step = 0.5
viscosity = 2.0
exact_products = lax.Precision.HIGHEST


def padded(cells, sides, width):
    for axis, dim in sides:
        count = lax.axis_size(axis)
        head = lax.slice_in_dim(cells, 0, width, axis=dim)
        tail = lax.slice_in_dim(cells, cells.shape[dim] - width, cells.shape[dim], axis=dim)
        cells = jnp.concatenate(
            [
                lax.ppermute(tail, axis, [(i, (i + 1) % count) for i in range(count)]),
                cells,
                lax.ppermute(head, axis, [((i + 1) % count, i) for i in range(count)]),
            ],
            axis=dim,
        )
    return cells


def peskin(gap):
    distance = jnp.abs(gap)
    inner_dist = jnp.minimum(distance, 1.0)
    outer_dist = jnp.clip(distance, 1.0, 2.0)
    near_part = (
        3.0 - 2.0 * inner_dist + jnp.sqrt(1.0 + 4.0 * inner_dist - 4.0 * inner_dist * inner_dist)
    ) / 8.0
    far_part = (
        5.0 - 2.0 * outer_dist - jnp.sqrt(-7.0 + 12.0 * outer_dist - 4.0 * outer_dist * outer_dist)
    ) / 8.0
    return jnp.where(distance < 1.0, near_part, far_part)


def kernel_rows(coords, first_node, node_count, shift, grid_cells):
    nodes = (first_node + jnp.arange(node_count, dtype=jnp.int32)).astype(jnp.float32) + shift
    gap = (
        jnp.mod(coords[:, None] - nodes[None, :] + 0.5 * grid_cells, grid_cells) - 0.5 * grid_cells
    )
    return peskin(gap)


def staggers(component):
    return [0.5 if axis_id == component else 0.0 for axis_id in range(3)]


def widen(field):
    return padded(field, (("gx", 1), ("gy", 2)), 2)


def interpolate(widened, places, x_first, y_first, grid_cells):
    sampled = []
    for component in range(3):
        shifts = staggers(component)
        weight_x = kernel_rows(places[0], x_first - 2, widened.shape[1], shifts[0], grid_cells)
        weight_y = kernel_rows(places[1], y_first - 2, widened.shape[2], shifts[1], grid_cells)
        weight_z = kernel_rows(places[2], 0, widened.shape[3], shifts[2], grid_cells)
        along_z = jnp.einsum("xyz,pz->pxy", widened[component], weight_z, precision=exact_products)
        along_y = jnp.einsum("pxy,py->px", along_z, weight_y, precision=exact_products)
        sampled.append(jnp.sum(along_y * weight_x, axis=1))
    return jnp.stack(sampled)


def twiddle(freq, length):
    columns = jnp.arange(length, dtype=jnp.int32)
    product = freq[:, None] * columns[None, :] % length
    angle = product.astype(jnp.float32) * (2.0 * math.pi / length)
    return (jnp.cos(angle), jnp.sin(angle))


def rotate(spectrum, table, form):
    return jnp.einsum(form, table, spectrum, precision=exact_products)


def block_table(cosine, sine, direction):
    return jnp.stack(
        [jnp.stack([cosine, direction * sine]), jnp.stack([-direction * sine, cosine])]
    )


def project_block(spectrum, freq_x, freq_y, freq_z, grid_cells):
    scale_angle = 2.0 * math.pi / grid_cells
    cos_x = jnp.cos(freq_x.astype(jnp.float32) * scale_angle)[:, None, None]
    sin_x = jnp.sin(freq_x.astype(jnp.float32) * scale_angle)[:, None, None]
    cos_y = jnp.cos(freq_y.astype(jnp.float32) * scale_angle)[None, :, None]
    sin_y = jnp.sin(freq_y.astype(jnp.float32) * scale_angle)[None, :, None]
    cos_z = jnp.cos(freq_z.astype(jnp.float32) * scale_angle)[None, None, :]
    sin_z = jnp.sin(freq_z.astype(jnp.float32) * scale_angle)[None, None, :]
    cos_list = [cos_x, cos_y, cos_z]
    sin_list = [sin_x, sin_y, sin_z]
    anchor = (
        (freq_x[:, None, None] == 0) & (freq_y[None, :, None] == 0) & (freq_z[None, None, :] == 0)
    ).astype(jnp.float32)
    laplace = 2.0 - 2.0 * cos_x + (2.0 - 2.0 * cos_y) + (2.0 - 2.0 * cos_z)
    inverse_lap = 1.0 / (laplace + anchor)
    damping = 1.0 / (1.0 + time_step * viscosity * laplace)
    real_in = spectrum[0]
    imag_in = spectrum[1]
    div_real = 0.0
    div_imag = 0.0
    for axis_id in range(3):
        div_real = (
            div_real
            + (1.0 - cos_list[axis_id]) * real_in[axis_id]
            - sin_list[axis_id] * imag_in[axis_id]
        )
        div_imag = (
            div_imag
            + (1.0 - cos_list[axis_id]) * imag_in[axis_id]
            + sin_list[axis_id] * real_in[axis_id]
        )
    real_out = []
    imag_out = []
    for axis_id in range(3):
        minus_one = cos_list[axis_id] - 1.0
        real_out.append(
            (real_in[axis_id] + (minus_one * div_real - sin_list[axis_id] * div_imag) * inverse_lap)
            * damping
        )
        imag_out.append(
            (imag_in[axis_id] + (minus_one * div_imag + sin_list[axis_id] * div_real) * inverse_lap)
            * damping
        )
    return jnp.stack([jnp.stack(real_out), jnp.stack(imag_out)])


def per_device(velocity, fluid_noise, cell, offset, colloid_velocity, particle_noise, counts):
    slab_cells = velocity.shape[1]
    pencil_cells = velocity.shape[2]
    grid_cells = velocity.shape[3]
    block_rows = cell.shape[1]
    x_first = lax.axis_index("gx") * slab_cells
    y_first = lax.axis_index("gy") * pencil_cells
    places = cell.astype(jnp.float32) + offset
    live = (jnp.arange(block_rows, dtype=jnp.int32) < counts[0]).astype(jnp.float32)
    sampled = interpolate(widen(velocity), places, x_first, y_first, grid_cells)
    colloid_force = live * (drag_rate * (colloid_velocity - sampled) + particle_noise)
    packed = jnp.concatenate([places, colloid_force], axis=0)
    nearby = padded(packed, (("gy", 1),), block_rows)
    spots = nearby[:3]
    loads = nearby[3:]
    layers = []
    for component in range(3):
        shifts = staggers(component)
        weight_x = kernel_rows(spots[0], x_first - 2, slab_cells + 4, shifts[0], grid_cells)
        weight_y = kernel_rows(spots[1], y_first, pencil_cells, shifts[1], grid_cells)
        weight_z = kernel_rows(spots[2], 0, grid_cells, shifts[2], grid_cells)
        plane = (weight_x[:, :, None] * weight_y[:, None, :]).reshape(
            spots.shape[1], (slab_cells + 4) * pencil_cells
        )
        loaded = weight_z * loads[component][:, None]
        layer = jnp.einsum("pa,pz->az", plane, loaded, precision=exact_products)
        layers.append(layer.reshape(slab_cells + 4, pencil_cells, grid_cells))
    spread_field = jnp.stack(layers)
    edge_layers = jnp.concatenate([spread_field[:, :2], spread_field[:, -2:]], axis=1)
    neighbours = padded(edge_layers, (("gx", 1),), 2)
    own_force = spread_field[:, 2:-2]
    own_force = own_force.at[:, :2].add(neighbours[:, :2])
    own_force = own_force.at[:, -2:].add(neighbours[:, -2:])
    rhs = velocity + time_step * own_force + fluid_noise
    freq_kept = jnp.arange(grid_cells, dtype=jnp.int32)
    keep_mask = jnp.ones((grid_cells,), jnp.float32)
    back_weight = jnp.ones((grid_cells,), jnp.float32)
    cos_depth, sin_depth = twiddle(freq_kept, grid_cells)
    forward_table = jnp.stack([cos_depth * keep_mask[:, None], -sin_depth * keep_mask[:, None]])
    spectrum = jnp.einsum("okz,cxyz->ocxyk", forward_table, rhs, precision=exact_products)
    freq_line = jnp.arange(grid_cells, dtype=jnp.int32)
    cos_line, sin_line = twiddle(freq_line, grid_cells)
    forward_block = block_table(cos_line, sin_line, 1.0)
    backward_block = block_table(cos_line, sin_line, -1.0)
    spectrum = lax.all_to_all(spectrum, "gy", split_axis=4, concat_axis=3, tiled=True)
    spectrum = rotate(spectrum, forward_block, "oiky,icxyz->ocxkz")
    spectrum = lax.all_to_all(spectrum, "gx", split_axis=3, concat_axis=2, tiled=True)
    spectrum = rotate(spectrum, forward_block, "oikx,icxyz->ockyz")
    local_y = spectrum.shape[3]
    local_z = spectrum.shape[4]
    freq_y = lax.axis_index("gx") * local_y + jnp.arange(local_y, dtype=jnp.int32)
    freq_z = lax.axis_index("gy") * local_z + jnp.arange(local_z, dtype=jnp.int32)
    spectrum = project_block(spectrum, freq_line, freq_y, freq_z, grid_cells)
    spectrum = rotate(spectrum, backward_block, "oikx,icxyz->ockyz")
    spectrum = lax.all_to_all(spectrum, "gx", split_axis=2, concat_axis=3, tiled=True)
    spectrum = rotate(spectrum, backward_block, "oiky,icxyz->ocxkz")
    spectrum = lax.all_to_all(spectrum, "gy", split_axis=3, concat_axis=4, tiled=True)
    norm_factor = 1.0 / float(grid_cells * grid_cells * grid_cells)
    scaled_weight = (back_weight * norm_factor)[:, None]
    back_table = jnp.stack([cos_depth * scaled_weight, -sin_depth * scaled_weight])
    new_velocity = jnp.einsum("ikz,icxyk->cxyz", back_table, spectrum, precision=exact_products)
    colloid_drift = live * interpolate(widen(new_velocity), places, x_first, y_first, grid_cells)
    return (new_velocity, colloid_force, colloid_drift)


def solution(mesh):
    placed = (
        P(None, "gx", "gy", None),
        P(None, "gx", "gy", None),
        P(None, ("gx", "gy")),
        P(None, ("gx", "gy")),
        P(None, ("gx", "gy")),
        P(None, ("gx", "gy")),
        P(("gx", "gy")),
    )
    return jax.shard_map(
        per_device,
        mesh=mesh,
        in_specs=placed,
        out_specs=(P(None, "gx", "gy", None), P(None, ("gx", "gy")), P(None, ("gx", "gy"))),
        check_vma=False,
    )
```

profile of v0, /device:TPU:0, one launch (start us, length us, event | category | flops | bytes accessed | tf_op | source)
XLA Modules:
  0.0 2014.4 jit_solution(7089020718572155720)
XLA Ops:
  2.4 2.9 collective-permute-start.1
  6.8 5.5 collective-permute-done
  12.4 4.0 constant_dynamic-update-slice_fusion.1
  16.6 3.1 collective-permute-start.2
  19.8 2.1 collective-permute-start.3
  22.1 6.5 collective-permute-done.2
  28.7 2.3 collective-permute-done.3
  32.5 2.5 fusion.78
  35.0 2.5 fusion.77
  37.6 2.5 fusion.76
  42.0 2.4 collective-permute-start.5
  46.6 5.0 fusion.52
  51.7 5.0 fusion.58
  56.7 5.5 fusion.55
  63.4 2.7 collective-permute-start.7
  67.0 5.8 collective-permute-done.6
  73.8 14.5 fusion.13
  88.3 32.0 %copy.82 = f32[2,3,32,64,256]{3,0,2,1,4:T(2,128)} copy(f32[2,3,32,64,256]{4,3,0,2,1:T(8,128)} %fusion.13) | data formatting | bytes 25165824 | tf_op jit(solution)/shard_map/okz,cxyz->ocxyk/transpose | solution.py:173
  120.2 32.4 %reshape.1211 = f32[4,1,786432]{2,1,0:T(1,128)} reshape(f32[256,3,32,2,64]{4,3,2,1,0:T(2,128)} %bitcast.336) | data formatting | bytes 25165824
  152.6 6.5 all-to-all-start
  161.3 272.1 %all-to-all-done = f32[4,1,786432]{2,1,0:T(1,128)} async-done(((f32[4,1,786432]{2,1,0:T(1,128)}), f32[4,1,786432]{2,1,0:T(1,128)}, u32[]{:S(2)}, u32[]{:S(2)}) %all-to-all-start) | async-done | bytes 12582944 | tf_op jit(solution)/shard_map/all_to_all | solution.py:178
  434.0 39.7 %reduce.28 = f32[4,786432]{1,0:T(4,128)} reduce(f32[4,1,786432]{2,1,0:T(1,128)} %all-to-all-done, f32[]{:T(128)} %broadcast.2479), dimensions={1}, to_apply=%all_to_all.52.reduce_sub_computation | reduce | bytes 25165828 | tf_op jit(solution)/shard_map/all_to_all | solution.py:178
  473.7 56.0 %reshape.1212 = f32[256,3,32,2,64]{4,3,2,1,0:T(2,128)} reshape(f32[4,786432]{1,0:T(4,128)} %reduce.28) | data formatting | bytes 25165824
  529.7 30.2 %copy.172 = f32[2,3,32,64,4,64]{3,4,5,0,2,1:T(4,128)} copy(f32[2,3,32,64,4,64]{3,0,2,1,5,4:T(2,128)} %bitcast.337) | data formatting | bytes 25165824 | tf_op jit(solution)/shard_map/all_to_all | solution.py:178
  559.9 23.2 %reshape.1186 = f32[2,3,32,256,64,1]{3,4,0,2,1,5:T(8,128)} reshape(f32[2,3,32,4,64,64]{4,3,5,0,2,1:T(4,128)} %bitcast.338) | data formatting | bytes 25165824 | tf_op jit(solution)/shard_map/all_to_all | solution.py:178
  583.1 24.8 %fusion.22 = f32[2,3,32,256,64]{3,4,0,2,1:T(8,128)} fusion(f32[2,3,32,256,64,1]{3,4,0,2,1,5:T(8,128)} %reshape.1186, f32[1,2,256,256]{3,2,1,0:T(8,128)S(1)} %get-tuple-element.60, f32[1,2,256,256]{3,2,1,0:T(8,128)S(1)} %get-tuple-element.63), kind=kOutput, calls=%fused_computation.24 | convolution fusion | flops 19327614976 | bytes 26214400 | tf_op jit(solution)/shard_map/oiky,icxyz->ocxkz/dot_general | solution.py:79
  607.9 32.0 %copy.84 = f32[2,3,32,256,64]{4,0,2,1,3:T(2,128)} copy(f32[2,3,32,256,64]{3,4,0,2,1:T(8,128)} %fusion.22) | data formatting | bytes 25165824 | tf_op jit(solution)/shard_map/oiky,icxyz->ocxkz/transpose | solution.py:79
  639.8 29.3 %reshape.1213 = f32[8,1,393216]{2,1,0:T(1,128)} reshape(f32[256,3,32,2,64]{4,3,2,1,0:T(2,128)} %bitcast.339) | data formatting | bytes 25165824
  669.2 5.3 all-to-all-start.1
  675.0 138.5 %all-to-all-done.1 = f32[8,1,393216]{2,1,0:T(1,128)} async-done(((f32[8,1,393216]{2,1,0:T(1,128)}), f32[8,1,393216]{2,1,0:T(1,128)}, u32[]{:S(2)}, u32[]{:S(2)}) %all-to-all-start.1) | async-done | bytes 12582944 | tf_op jit(solution)/shard_map/all_to_all | solution.py:180
  813.5 37.1 %reduce.29 = f32[8,393216]{1,0:T(8,128)} reduce(f32[8,1,393216]{2,1,0:T(1,128)} %all-to-all-done.1, f32[]{:T(128)} %broadcast.2479), dimensions={1}, to_apply=%all_to_all.56.reduce_sub_computation | reduce | bytes 25165828 | tf_op jit(solution)/shard_map/all_to_all | solution.py:180
  850.6 41.7 %reshape.1214 = f32[256,3,32,2,64]{4,3,2,1,0:T(2,128)} reshape(f32[8,393216]{1,0:T(8,128)} %reduce.29) | data formatting | bytes 25165824
  892.3 24.9 %copy.85 = f32[2,3,32,256,64]{4,3,2,1,0:T(8,128)} copy(f32[2,3,32,256,64]{4,0,2,1,3:T(2,128)} %bitcast.340) | data formatting | bytes 25165824 | tf_op jit(solution)/shard_map/all_to_all | solution.py:180
  917.2 9.9 copy.86
  927.1 113.1 %fusion.16 = f32[2,3,256,32,64]{2,4,0,3,1:T(8,128)} fusion(f32[2,3,256,32,64,1]{4,3,2,1,0,5:T(8,128)S(1)} %bitcast.334, f32[1,2,256,256]{3,2,1,0:T(8,128)S(1)} %get-tuple-element.60, f32[1,2,256,256]{3,2,1,0:T(8,128)S(1)} %get-tuple-element.63), kind=kOutput, calls=%fused_computation.22 | convolution fusion | flops 19327614976 | bytes 26214400 | tf_op jit(solution)/shard_map/oikx,icxyz->ockyz/dot_general | solution.py:79
  1040.2 6.1 add_multiply_fusion.5
  1046.3 2.1 copy-done
  1048.4 3.3 add_multiply_fusion.4
  1053.4 22.8 %fusion.25 = f32[2,3,256,32,64]{2,4,0,3,1:T(8,128)} fusion(f32[1,2,256,256]{3,2,1,0:T(8,128)S(1)} %copy-done.3, f32[1,2,256,256]{3,2,1,0:T(8,128)S(1)} %copy-done.2, f32[1,3,256,32,64]{2,4,3,1,0:T(8,128)S(1)} %maximum_bitcast_fusion.2, f32[1,3,256,32,64]{2,4,3,1,0:T(8,128)S(1)} %maximum_bitcast_fusion.1), kind=kOutput, calls=%fused_computation.25 | convolution fusion | flops 19330760704 | bytes 26214400 | tf_op jit(solution)/shard_map/oikx,icxyz->ockyz/dot_general | solution.py:79
  1076.2 32.0 %copy.94 = f32[2,3,256,32,64]{4,0,3,1,2:T(2,128)} copy(f32[2,3,256,32,64]{2,4,0,3,1:T(8,128)} %fusion.25) | data formatting | bytes 25165824 | tf_op jit(solution)/shard_map/oikx,icxyz->ockyz/transpose | solution.py:79
  1108.2 29.7 %reshape.1215 = f32[8,1,393216]{2,1,0:T(1,128)} reshape(f32[256,3,32,2,64]{4,3,2,1,0:T(2,128)} %bitcast.342) | data formatting | bytes 25165824
  1137.9 145.6 %all_to_all.72 = f32[8,1,393216]{2,1,0:T(1,128)} all-to-all(f32[8,1,393216]{2,1,0:T(1,128)} %reshape.1215), channel_id=1, replica_groups=mesh['gx'=8,'gy'=4] {'gx'}, dimensions={0} | all-to-all | bytes 25165824 | tf_op jit(solution)/shard_map/all_to_all | solution.py:188
  1283.6 36.7 %reduce.30 = f32[8,393216]{1,0:T(8,128)} reduce(f32[8,1,393216]{2,1,0:T(1,128)} %all_to_all.72, f32[]{:T(128)} %broadcast.2479), dimensions={1}, to_apply=%all_to_all.60.reduce_sub_computation | reduce | bytes 25165828 | tf_op jit(solution)/shard_map/all_to_all | solution.py:188
  1320.3 41.7 %reshape.1216 = f32[256,3,32,2,64]{4,3,2,1,0:T(2,128)} reshape(f32[8,393216]{1,0:T(8,128)} %reduce.30) | data formatting | bytes 25165824
  1362.0 19.0 copy.95
  1381.0 9.9 copy.96
  1390.8 83.5 %fusion.19 = f32[2,3,32,256,64]{3,4,0,2,1:T(8,128)} fusion(f32[2,3,32,256,64,1]{4,3,2,1,0,5:T(8,128)S(1)} %bitcast.335, f32[1,2,256,256]{3,2,1,0:T(8,128)S(1)} %copy-done.3, f32[1,2,256,256]{3,2,1,0:T(8,128)S(1)} %copy-done.2), kind=kOutput, calls=%fused_computation.23 | convolution fusion | flops 19327614976 | bytes 26214400 | tf_op jit(solution)/shard_map/oiky,icxyz->ocxkz/dot_general | solution.py:79
  1474.4 32.0 %copy.98 = f32[2,3,32,256,64]{4,0,2,1,3:T(2,128)} copy(f32[2,3,32,256,64]{3,4,0,2,1:T(8,128)} %fusion.19) | data formatting | bytes 25165824 | tf_op jit(solution)/shard_map/oiky,icxyz->ocxkz/transpose | solution.py:79
  1506.3 32.4 %reshape.1217 = f32[4,1,786432]{2,1,0:T(1,128)} reshape(f32[256,3,32,2,64]{4,3,2,1,0:T(2,128)} %bitcast.345) | data formatting | bytes 25165824
  1538.7 6.3 all-to-all-start.3
  1546.1 271.6 %all-to-all-done.3 = f32[4,1,786432]{2,1,0:T(1,128)} async-done(((f32[4,1,786432]{2,1,0:T(1,128)}), f32[4,1,786432]{2,1,0:T(1,128)}, u32[]{:S(2)}, u32[]{:S(2)}) %all-to-all-start.3) | async-done | bytes 12582944 | tf_op jit(solution)/shard_map/all_to_all | solution.py:190
  1817.7 39.9 %reduce.31 = f32[4,786432]{1,0:T(4,128)} reduce(f32[4,1,786432]{2,1,0:T(1,128)} %all-to-all-done.3, f32[]{:T(128)} %broadcast.2479), dimensions={1}, to_apply=%all_to_all.64.reduce_sub_computation | reduce | bytes 25165828 | tf_op jit(solution)/shard_map/all_to_all | solution.py:190
  1857.7 56.0 %reshape.1218 = f32[256,3,32,2,64]{4,3,2,1,0:T(2,128)} reshape(f32[4,786432]{1,0:T(4,128)} %reduce.31) | data formatting | bytes 25165824
  1913.6 30.2 %copy.171 = f32[2,3,32,4,64,64]{5,3,4,0,2,1:T(4,128)} copy(f32[2,3,32,4,64,64]{5,0,2,1,4,3:T(2,128)} %bitcast.346) | data formatting | bytes 25165824 | tf_op jit(solution)/shard_map/all_to_all | solution.py:190
  1943.8 23.2 %all_to_all.67 = f32[2,3,32,64,256]{4,3,0,2,1:T(8,128)} reshape(f32[2,3,32,64,4,64]{5,4,3,0,2,1:T(4,128)} %bitcast.347) | data formatting | bytes 25165824 | tf_op jit(solution)/shard_map/all_to_all | solution.py:190
  1967.0 13.2 convolution_bitcast_fusion
  1980.4 2.8 collective-permute-start.9
  1983.2 8.8 collective-permute-done.8
  1992.3 3.8 collective-permute-start.11
  1996.1 6.2 collective-permute-done.10
  2002.3 2.0 collective-permute-done.11
  2005.7 2.5 fusion.75
  2008.3 2.5 fusion.73
  2010.8 2.6 fusion.74
  (121 shorter events, 19.9 us)
Async XLA Ops:
  1.8 10.5 collective-permute-start
  2.4 14.0 collective-permute-start.1
  5.3 51.4 %copy-start.11 = (f32[256]{0:T(256)}, f32[256]{0:T(256)S(1)}, u32[]{:S(2)}) copy-start(f32[256]{0:T(256)S(1)} %iota_convert_fusion) | copy-start | bytes 3076
  5.3 46.3 %copy-start.19 = (f32[256]{0:T(256)}, f32[256]{0:T(256)S(1)}, u32[]{:S(2)}) copy-start(f32[256]{0:T(256)S(1)} %fusion.383) | copy-start | bytes 3076
  5.4 40.5 %copy-start.13 = (f32[36]{0:T(128)}, f32[36]{0:T(128)S(1)}, u32[]{:S(2)}) copy-start(f32[36]{0:T(128)S(1)} %add_convert_fusion) | copy-start | bytes 436
  5.4 40.5 %copy-start.15 = (f32[36]{0:T(128)}, f32[36]{0:T(128)S(1)}, u32[]{:S(2)}) copy-start(f32[36]{0:T(128)S(1)} %broadcast_add_fusion.5) | copy-start | bytes 436
  6.1 34.2 %copy-start.23 = (f32[128]{0:T(128)}, f32[128]{0:T(128)S(1)}, u32[]{:S(2)}) copy-start(f32[128]{0:T(128)S(1)} %compare_convert_fusion) | copy-start | bytes 1540
  6.8 30.7 %copy-start.9 = (f32[128]{0:T(128)}, f32[128]{0:T(128)S(1)}, u32[]{:S(2)}) copy-start(f32[128]{0:T(128)S(1)} %get-tuple-element.71) | copy-start | bytes 1540
  6.8 33.3 %copy-start.17 = (f32[128]{0:T(128)}, f32[128]{0:T(128)S(1)}, u32[]{:S(2)}) copy-start(f32[128]{0:T(128)S(1)} %get-tuple-element.69) | copy-start | bytes 1540
  16.6 12.0 collective-permute-start.2
  19.8 11.2 collective-permute-start.3
  22.1 12.9 copy-start.6
  22.1 15.5 copy-start.4
  32.4 7.9 copy-start.21
  32.4 7.9 copy-start.22
  40.3 6.3 copy-start.8
  40.4 5.5 collective-permute-start.4
  42.0 3.8 collective-permute-start.5
  62.3 10.5 collective-permute-start.6
  63.4 10.3 collective-permute-start.7
  66.1 7.7 slice-start
  66.5 7.2 slice-start.1
  152.6 280.8 %all-to-all-start = ((f32[4,1,786432]{2,1,0:T(1,128)}), f32[4,1,786432]{2,1,0:T(1,128)}, u32[]{:S(2)}, u32[]{:S(2)}) async-start(f32[4,1,786432]{2,1,0:T(1,128)} %reshape.1211), calls=%async_computation | async-start | bytes 25165824 | tf_op jit(solution)/shard_map/all_to_all | solution.py:178
  669.2 144.3 %all-to-all-start.1 = ((f32[8,1,393216]{2,1,0:T(1,128)}), f32[8,1,393216]{2,1,0:T(1,128)}, u32[]{:S(2)}, u32[]{:S(2)}) async-start(f32[8,1,393216]{2,1,0:T(1,128)} %reshape.1213), calls=%async_computation.1 | async-start | bytes 25165824 | tf_op jit(solution)/shard_map/all_to_all | solution.py:180
  1040.2 8.3 copy-start
  1052.2 1.0 copy-start.2
  1052.2 1.2 copy-start.3
  1538.7 279.0 %all-to-all-start.3 = ((f32[4,1,786432]{2,1,0:T(1,128)}), f32[4,1,786432]{2,1,0:T(1,128)}, u32[]{:S(2)}, u32[]{:S(2)}) async-start(f32[4,1,786432]{2,1,0:T(1,128)} %reshape.1217), calls=%async_computation.3 | async-start | bytes 25165824 | tf_op jit(solution)/shard_map/all_to_all | solution.py:190
  1980.2 24.0 %copy-start.1 = (f32[3,32,64,256]{3,2,1,0:T(8,128)}, f32[3,32,64,256]{3,2,1,0:T(8,128)S(1)}, u32[]{:S(2)}) copy-start(f32[3,32,64,256]{3,2,1,0:T(8,128)S(1)} %convolution_bitcast_fusion) | copy-start | bytes 18874372
  1980.3 11.7 collective-permute-start.8
  1980.4 11.6 collective-permute-start.9
  1992.2 10.2 collective-permute-start.10
  1992.2 13.4 copy-start.5
  1992.2 13.4 copy-start.10
  1992.3 13.4 copy-start.12
  1992.3 16.0 copy-start.20
  1992.3 12.0 collective-permute-start.11
  2005.6 5.2 copy-start.7
  2005.7 7.7 copy-start.14
  2005.7 7.7 copy-start.16
  2005.7 7.7 copy-start.18
  2005.7 7.9 copy-start.24
where the time goes:
time: 2030 us; the launch traced here: 2010 us
  waiting for transfers between devices  721 us (36%)
  local copies, waits for them, and re-layouts  627 us (31%)
  matrix products  303 us (15%)
  other arithmetic  175 us (9%)
  blocking collectives  146 us (7%)
  starting transfers between devices  40.4 us (2%)
    unnamed x64, local copies, waits for them, and re-layouts  326 us
    all_to_all x1, waiting for transfers between devices, per_device(): lax.all_to_all(spectrum, 'gy', split_axis=4, concat_axis=3, tiled=True)  272 us
    all_to_all x1, waiting for transfers between devices, per_device(): lax.all_to_all(spectrum, 'gy', split_axis=3, concat_axis=4, tiled=True)  272 us
    dot_general x4, matrix products, rotate(): return jnp.einsum(form, table, spectrum, precision=exact_products)  244 us
    all_to_all x1, blocking collectives, per_device(): lax.all_to_all(spectrum, 'gx', split_axis=2, concat_axis=3, tiled=True)  146 us
    all_to_all x1, waiting for transfers between devices, per_device(): lax.all_to_all(spectrum, 'gx', split_axis=3, concat_axis=2, tiled=True)  138 us
    transpose x3, local copies, waits for them, and re-layouts, rotate(): return jnp.einsum(form, table, spectrum, precision=exact_products)  95.9 us
    all_to_all x3, local copies, waits for them, and re-layouts, per_device(): lax.all_to_all(spectrum, 'gy', split_axis=4, concat_axis=3, tiled=True)  54 us
  transfers between devices with their start and end apart: 15, of which 12 were waited for; matrix products, arithmetic and copies ran while one was open for 1% of the time, Pallas kernels for 0%

commit v1 on v0

--- a/solution.py
+++ b/solution.py
@@ -175,7 +175,10 @@
     cos_line, sin_line = twiddle(freq_line, grid_cells)
     forward_block = block_table(cos_line, sin_line, 1.0)
     backward_block = block_table(cos_line, sin_line, -1.0)
-    spectrum = lax.all_to_all(spectrum, "gy", split_axis=4, concat_axis=3, tiled=True)
+    spectrum = jnp.concatenate(
+        lax.all_to_all(jnp.stack(jnp.split(spectrum, lax.axis_size("gy"), axis=4)), "gy", 0, 0),
+        axis=3,
+    )
     spectrum = rotate(spectrum, forward_block, "oiky,icxyz->ocxkz")
     spectrum = lax.all_to_all(spectrum, "gx", split_axis=3, concat_axis=2, tiled=True)
     spectrum = rotate(spectrum, forward_block, "oikx,icxyz->ockyz")

time: 2030 us -> 2020 us (level)
  local copies, waits for them, and re-layouts: 627 us -> 604 us
    reshape x0 -> x3, local copies, waits for them, and re-layouts: none -> 69.4 us  [per_device(): jnp.concatenate(lax.all_to_all(jnp.stack(jnp.split(spectrum, lax.axis_siz...]
    all_to_all x3 -> x1, local copies, waits for them, and re-layouts: 54 us -> 0.59 us  [per_device(): lax.all_to_all(jnp.stack(jnp.split(spectrum, lax.axis_size('gy'), axis=4)...]
    transpose x1 -> x0, local copies, waits for them, and re-layouts: 32 us -> none  [per_device(): jnp.einsum('okz,cxyz->ocxyk', forward_table, rhs, precision=exact_products)]
    unnamed x64, local copies, waits for them, and re-layouts: 326 us -> 304 us
where the time goes in v1:
time: 2020 us; the launch traced here: 2010 us
  waiting for transfers between devices  722 us (36%)
  local copies, waits for them, and re-layouts  604 us (30%)
  matrix products  302 us (15%)
  other arithmetic  191 us (9%)
  blocking collectives  146 us (7%)
  starting transfers between devices  40.4 us (2%)
    unnamed x64, local copies, waits for them, and re-layouts  304 us
    all_to_all x1, waiting for transfers between devices, per_device(): lax.all_to_all(jnp.stack(jnp.split(spectrum, lax.axis_size('gy'), axis=4)...  272 us
    all_to_all x1, waiting for transfers between devices, per_device(): lax.all_to_all(spectrum, 'gy', split_axis=3, concat_axis=4, tiled=True)  272 us
    dot_general x4, matrix products, rotate(): return jnp.einsum(form, table, spectrum, precision=exact_products)  244 us
    all_to_all x1, blocking collectives, per_device(): lax.all_to_all(spectrum, 'gx', split_axis=2, concat_axis=3, tiled=True)  146 us
    all_to_all x1, waiting for transfers between devices, per_device(): lax.all_to_all(spectrum, 'gx', split_axis=3, concat_axis=2, tiled=True)  138 us
    transpose x3, local copies, waits for them, and re-layouts, rotate(): return jnp.einsum(form, table, spectrum, precision=exact_products)  95.8 us
    reshape x3, local copies, waits for them, and re-layouts, per_device(): jnp.concatenate(lax.all_to_all(jnp.stack(jnp.split(spectrum, lax.axis_siz...  69.4 us
  transfers between devices with their start and end apart: 15, of which 12 were waited for; matrix products, arithmetic and copies ran while one was open for 1% of the time, Pallas kernels for 0%

profile of v1, /device:TPU:0, one launch (start us, length us, event | category | flops | bytes accessed | tf_op | source)
XLA Modules:
  0.0 2007.1 jit_solution(12043265142980597526)
XLA Ops:
  2.4 2.9 collective-permute-start.1
  6.8 5.5 collective-permute-done
  12.4 4.0 constant_dynamic-update-slice_fusion.1
  16.6 3.1 collective-permute-start.2
  22.1 6.5 collective-permute-done.2
  28.7 2.3 collective-permute-done.3
  32.5 2.5 fusion.78
  35.0 2.5 fusion.77
  37.6 2.5 fusion.76
  42.0 2.4 collective-permute-start.5
  46.6 5.0 fusion.52
  51.7 5.0 fusion.58
  56.7 5.5 fusion.55
  64.1 2.7 collective-permute-start.7
  67.7 6.2 collective-permute-done.6
  74.7 14.4 fusion.13
  89.1 15.3 slice_bitcast_fusion.3
  104.4 16.0 fusion.509
  120.4 33.5 %reshape.1220 = f32[4,1,786432]{2,1,0:T(1,128)} reshape(f32[4,3,32,2,64,64]{5,4,3,2,1,0:T(8,128)} %fusion.509) | data formatting | bytes 25165824
  153.9 6.5 all-to-all-start
  162.5 272.1 %all-to-all-done = f32[4,1,786432]{2,1,0:T(1,128)} async-done(((f32[4,1,786432]{2,1,0:T(1,128)}), f32[4,1,786432]{2,1,0:T(1,128)}, u32[]{:S(2)}, u32[]{:S(2)}) %all-to-all-start) | async-done | bytes 12582944 | tf_op jit(solution)/shard_map/all_to_all | solution.py:179
  435.2 39.6 %reduce.28 = f32[4,786432]{1,0:T(4,128)} reduce(f32[4,1,786432]{2,1,0:T(1,128)} %all-to-all-done, f32[]{:T(128)} %broadcast.2479), dimensions={1}, to_apply=%all_to_all.42.reduce_sub_computation | reduce | bytes 25165828 | tf_op jit(solution)/shard_map/all_to_all | solution.py:179
  474.8 32.1 %reshape.1221 = f32[4,3,32,2,64,64]{5,4,3,2,1,0:T(8,128)} reshape(f32[4,786432]{1,0:T(4,128)} %reduce.28) | data formatting | bytes 25165824
  506.9 17.6 bitcast_bitcast_fusion
  524.5 28.6 %copy.144 = f32[2,3,32,4,64,64]{4,3,5,0,2,1:T(4,128)} copy(f32[2,3,32,4,64,64]{5,4,0,2,1,3:T(8,128)} %bitcast_bitcast_fusion) | data formatting | bytes 25165824 | tf_op jit(solution)/shard_map/reshape | solution.py:178
  553.1 23.2 %reshape.1194 = f32[2,3,32,256,64,1]{3,4,0,2,1,5:T(8,128)} reshape(f32[2,3,32,4,64,64]{4,3,5,0,2,1:T(4,128)} %copy.144) | data formatting | bytes 25165824 | tf_op jit(solution)/shard_map/reshape | solution.py:178
  576.3 24.3 %fusion.22 = f32[2,3,32,256,64]{3,4,0,2,1:T(8,128)} fusion(f32[2,3,32,256,64,1]{3,4,0,2,1,5:T(8,128)} %reshape.1194, f32[1,2,256,256]{3,2,1,0:T(8,128)S(1)} %get-tuple-element.64, f32[1,2,256,256]{3,2,1,0:T(8,128)S(1)} %get-tuple-element.67), kind=kOutput, calls=%fused_computation.28 | convolution fusion | flops 19327614976 | bytes 26214400 | tf_op jit(solution)/shard_map/oiky,icxyz->ocxkz/dot_general | solution.py:79
  600.6 31.9 %copy.84 = f32[2,3,32,256,64]{4,0,2,1,3:T(2,128)} copy(f32[2,3,32,256,64]{3,4,0,2,1:T(8,128)} %fusion.22) | data formatting | bytes 25165824 | tf_op jit(solution)/shard_map/oiky,icxyz->ocxkz/transpose | solution.py:79
  632.6 29.3 %reshape.1222 = f32[8,1,393216]{2,1,0:T(1,128)} reshape(f32[256,3,32,2,64]{4,3,2,1,0:T(2,128)} %bitcast.344) | data formatting | bytes 25165824
  661.9 5.3 all-to-all-start.1
  667.8 138.5 %all-to-all-done.1 = f32[8,1,393216]{2,1,0:T(1,128)} async-done(((f32[8,1,393216]{2,1,0:T(1,128)}), f32[8,1,393216]{2,1,0:T(1,128)}, u32[]{:S(2)}, u32[]{:S(2)}) %all-to-all-start.1) | async-done | bytes 12582944 | tf_op jit(solution)/shard_map/all_to_all | solution.py:183
  806.2 36.9 %reduce.29 = f32[8,393216]{1,0:T(8,128)} reduce(f32[8,1,393216]{2,1,0:T(1,128)} %all-to-all-done.1, f32[]{:T(128)} %broadcast.2479), dimensions={1}, to_apply=%all_to_all.43.reduce_sub_computation | reduce | bytes 25165828 | tf_op jit(solution)/shard_map/all_to_all | solution.py:183
  843.2 41.8 %reshape.1223 = f32[256,3,32,2,64]{4,3,2,1,0:T(2,128)} reshape(f32[8,393216]{1,0:T(8,128)} %reduce.29) | data formatting | bytes 25165824
  885.0 24.9 %copy.85 = f32[2,3,32,256,64]{4,3,2,1,0:T(8,128)} copy(f32[2,3,32,256,64]{4,0,2,1,3:T(2,128)} %bitcast.345) | data formatting | bytes 25165824 | tf_op jit(solution)/shard_map/all_to_all | solution.py:183
  909.9 9.9 copy.86
  919.7 113.2 %fusion.16 = f32[2,3,256,32,64]{2,4,0,3,1:T(8,128)} fusion(f32[2,3,256,32,64,1]{4,3,2,1,0,5:T(8,128)S(1)} %bitcast.342, f32[1,2,256,256]{3,2,1,0:T(8,128)S(1)} %get-tuple-element.64, f32[1,2,256,256]{3,2,1,0:T(8,128)S(1)} %get-tuple-element.67), kind=kOutput, calls=%fused_computation.26 | convolution fusion | flops 19327614976 | bytes 26214400 | tf_op jit(solution)/shard_map/oikx,icxyz->ockyz/dot_general | solution.py:79
  1033.0 6.1 add_multiply_fusion.5
  1039.1 2.1 copy-done
  1041.2 3.3 add_multiply_fusion.4
  1046.2 22.8 %fusion.25 = f32[2,3,256,32,64]{2,4,0,3,1:T(8,128)} fusion(f32[1,2,256,256]{3,2,1,0:T(8,128)S(1)} %copy-done.3, f32[1,2,256,256]{3,2,1,0:T(8,128)S(1)} %copy-done.2, f32[1,3,256,32,64]{2,4,3,1,0:T(8,128)S(1)} %maximum_bitcast_fusion.2, f32[1,3,256,32,64]{2,4,3,1,0:T(8,128)S(1)} %maximum_bitcast_fusion.1), kind=kOutput, calls=%fused_computation.29 | convolution fusion | flops 19330760704 | bytes 26214400 | tf_op jit(solution)/shard_map/oikx,icxyz->ockyz/dot_general | solution.py:79
  1069.0 31.9 %copy.94 = f32[2,3,256,32,64]{4,0,3,1,2:T(2,128)} copy(f32[2,3,256,32,64]{2,4,0,3,1:T(8,128)} %fusion.25) | data formatting | bytes 25165824 | tf_op jit(solution)/shard_map/oikx,icxyz->ockyz/transpose | solution.py:79
  1100.9 29.7 %reshape.1224 = f32[8,1,393216]{2,1,0:T(1,128)} reshape(f32[256,3,32,2,64]{4,3,2,1,0:T(2,128)} %bitcast.347) | data formatting | bytes 25165824
  1130.6 145.7 %all_to_all.59 = f32[8,1,393216]{2,1,0:T(1,128)} all-to-all(f32[8,1,393216]{2,1,0:T(1,128)} %reshape.1224), channel_id=1, replica_groups=mesh['gx'=8,'gy'=4] {'gx'}, dimensions={0} | all-to-all | bytes 25165824 | tf_op jit(solution)/shard_map/all_to_all | solution.py:191
  1276.3 36.7 %reduce.30 = f32[8,393216]{1,0:T(8,128)} reduce(f32[8,1,393216]{2,1,0:T(1,128)} %all_to_all.59, f32[]{:T(128)} %broadcast.2479), dimensions={1}, to_apply=%all_to_all.47.reduce_sub_computation | reduce | bytes 25165828 | tf_op jit(solution)/shard_map/all_to_all | solution.py:191
  1313.0 41.7 %reshape.1225 = f32[256,3,32,2,64]{4,3,2,1,0:T(2,128)} reshape(f32[8,393216]{1,0:T(8,128)} %reduce.30) | data formatting | bytes 25165824
  1354.7 19.0 copy.95
  1373.7 9.9 copy.96
  1383.6 83.5 %fusion.19 = f32[2,3,32,256,64]{3,4,0,2,1:T(8,128)} fusion(f32[2,3,32,256,64,1]{4,3,2,1,0,5:T(8,128)S(1)} %bitcast.343, f32[1,2,256,256]{3,2,1,0:T(8,128)S(1)} %copy-done.3, f32[1,2,256,256]{3,2,1,0:T(8,128)S(1)} %copy-done.2), kind=kOutput, calls=%fused_computation.27 | convolution fusion | flops 19327614976 | bytes 26214400 | tf_op jit(solution)/shard_map/oiky,icxyz->ocxkz/dot_general | solution.py:79
  1467.1 32.0 %copy.98 = f32[2,3,32,256,64]{4,0,2,1,3:T(2,128)} copy(f32[2,3,32,256,64]{3,4,0,2,1:T(8,128)} %fusion.19) | data formatting | bytes 25165824 | tf_op jit(solution)/shard_map/oiky,icxyz->ocxkz/transpose | solution.py:79
  1499.0 32.4 %reshape.1226 = f32[4,1,786432]{2,1,0:T(1,128)} reshape(f32[256,3,32,2,64]{4,3,2,1,0:T(2,128)} %bitcast.350) | data formatting | bytes 25165824
  1531.4 6.3 all-to-all-start.3
  1538.8 271.6 %all-to-all-done.3 = f32[4,1,786432]{2,1,0:T(1,128)} async-done(((f32[4,1,786432]{2,1,0:T(1,128)}), f32[4,1,786432]{2,1,0:T(1,128)}, u32[]{:S(2)}, u32[]{:S(2)}) %all-to-all-start.3) | async-done | bytes 12582944 | tf_op jit(solution)/shard_map/all_to_all | solution.py:193
  1810.4 39.9 %reduce.31 = f32[4,786432]{1,0:T(4,128)} reduce(f32[4,1,786432]{2,1,0:T(1,128)} %all-to-all-done.3, f32[]{:T(128)} %broadcast.2479), dimensions={1}, to_apply=%all_to_all.51.reduce_sub_computation | reduce | bytes 25165828 | tf_op jit(solution)/shard_map/all_to_all | solution.py:193
  1850.3 56.0 %reshape.1227 = f32[256,3,32,2,64]{4,3,2,1,0:T(2,128)} reshape(f32[4,786432]{1,0:T(4,128)} %reduce.31) | data formatting | bytes 25165824
  1906.3 30.2 %copy.172 = f32[2,3,32,4,64,64]{5,3,4,0,2,1:T(4,128)} copy(f32[2,3,32,4,64,64]{5,0,2,1,4,3:T(2,128)} %bitcast.351) | data formatting | bytes 25165824 | tf_op jit(solution)/shard_map/all_to_all | solution.py:193
  1936.5 23.2 %all_to_all.54 = f32[2,3,32,64,256]{4,3,0,2,1:T(8,128)} reshape(f32[2,3,32,64,4,64]{5,4,3,0,2,1:T(4,128)} %bitcast.352) | data formatting | bytes 25165824 | tf_op jit(solution)/shard_map/all_to_all | solution.py:193
  1959.7 13.2 convolution_bitcast_fusion
  1973.1 2.8 collective-permute-start.9
  1975.9 8.8 collective-permute-done.8
  1985.0 3.8 collective-permute-start.11
  1988.8 6.2 collective-permute-done.10
  1998.4 2.5 fusion.75
  2001.0 2.6 fusion.73
  2003.5 2.6 fusion.74
  (123 shorter events, 24.4 us)
Async XLA Ops:
  1.8 10.5 collective-permute-start
  2.4 14.0 collective-permute-start.1
  5.3 51.4 %copy-start.11 = (f32[256]{0:T(256)}, f32[256]{0:T(256)S(1)}, u32[]{:S(2)}) copy-start(f32[256]{0:T(256)S(1)} %iota_convert_fusion) | copy-start | bytes 3076
  5.3 46.3 %copy-start.19 = (f32[256]{0:T(256)}, f32[256]{0:T(256)S(1)}, u32[]{:S(2)}) copy-start(f32[256]{0:T(256)S(1)} %fusion.383) | copy-start | bytes 3076
  5.4 40.5 %copy-start.13 = (f32[36]{0:T(128)}, f32[36]{0:T(128)S(1)}, u32[]{:S(2)}) copy-start(f32[36]{0:T(128)S(1)} %add_convert_fusion) | copy-start | bytes 436
  5.4 40.5 %copy-start.15 = (f32[36]{0:T(128)}, f32[36]{0:T(128)S(1)}, u32[]{:S(2)}) copy-start(f32[36]{0:T(128)S(1)} %broadcast_add_fusion.5) | copy-start | bytes 436
  6.1 34.2 %copy-start.23 = (f32[128]{0:T(128)}, f32[128]{0:T(128)S(1)}, u32[]{:S(2)}) copy-start(f32[128]{0:T(128)S(1)} %compare_convert_fusion) | copy-start | bytes 1540
  6.8 30.7 %copy-start.9 = (f32[128]{0:T(128)}, f32[128]{0:T(128)S(1)}, u32[]{:S(2)}) copy-start(f32[128]{0:T(128)S(1)} %get-tuple-element.75) | copy-start | bytes 1540
  6.8 33.3 %copy-start.17 = (f32[128]{0:T(128)}, f32[128]{0:T(128)S(1)}, u32[]{:S(2)}) copy-start(f32[128]{0:T(128)S(1)} %get-tuple-element.73) | copy-start | bytes 1540
  16.6 12.0 collective-permute-start.2
  19.8 11.2 collective-permute-start.3
  22.1 12.9 copy-start.6
  22.1 15.5 copy-start.4
  32.4 7.9 copy-start.21
  32.4 7.9 copy-start.22
  40.3 6.3 copy-start.8
  40.4 5.5 collective-permute-start.4
  42.0 3.8 collective-permute-start.5
  63.0 10.9 collective-permute-start.6
  64.1 10.5 collective-permute-start.7
  66.8 7.9 slice-start
  67.2 7.4 slice-start.1
  153.9 280.8 %all-to-all-start = ((f32[4,1,786432]{2,1,0:T(1,128)}), f32[4,1,786432]{2,1,0:T(1,128)}, u32[]{:S(2)}, u32[]{:S(2)}) async-start(f32[4,1,786432]{2,1,0:T(1,128)} %reshape.1220), calls=%async_computation | async-start | bytes 25165824 | tf_op jit(solution)/shard_map/all_to_all | solution.py:179
  661.9 144.3 %all-to-all-start.1 = ((f32[8,1,393216]{2,1,0:T(1,128)}), f32[8,1,393216]{2,1,0:T(1,128)}, u32[]{:S(2)}, u32[]{:S(2)}) async-start(f32[8,1,393216]{2,1,0:T(1,128)} %reshape.1222), calls=%async_computation.1 | async-start | bytes 25165824 | tf_op jit(solution)/shard_map/all_to_all | solution.py:183
  1032.9 8.3 copy-start
  1045.0 1.0 copy-start.2
  1045.0 1.2 copy-start.3
  1531.4 279.0 %all-to-all-start.3 = ((f32[4,1,786432]{2,1,0:T(1,128)}), f32[4,1,786432]{2,1,0:T(1,128)}, u32[]{:S(2)}, u32[]{:S(2)}) async-start(f32[4,1,786432]{2,1,0:T(1,128)} %reshape.1226), calls=%async_computation.3 | async-start | bytes 25165824 | tf_op jit(solution)/shard_map/all_to_all | solution.py:193
  1972.9 24.0 %copy-start.1 = (f32[3,32,64,256]{3,2,1,0:T(8,128)}, f32[3,32,64,256]{3,2,1,0:T(8,128)S(1)}, u32[]{:S(2)}) copy-start(f32[3,32,64,256]{3,2,1,0:T(8,128)S(1)} %convolution_bitcast_fusion) | copy-start | bytes 18874372
  1973.0 11.7 collective-permute-start.8
  1973.1 11.6 collective-permute-start.9
  1984.9 10.2 collective-permute-start.10
  1984.9 13.4 copy-start.5
  1985.0 13.4 copy-start.10
  1985.0 13.4 copy-start.12
  1985.0 16.0 copy-start.20
  1985.0 12.0 collective-permute-start.11
  1998.3 5.2 copy-start.7
  1998.4 7.7 copy-start.14
  1998.4 7.7 copy-start.16
  1998.4 7.7 copy-start.18
  1998.4 7.9 copy-start.24
